TPU v7x, 128 devices: a whole 4x4x4 slice. The times are simulated.
128 devices in a mesh: comp: 2 (over core), rank: 64 (over y, x, z).
Axes of the slice: x: 4, y: 4, z: 4, core: 2. Of those that a mesh axis runs over, the one named last changes fastest.
Arguments:
- surface_fields: bfloat16 [2, 40, 262144], P('comp', None, 'rank'), may hold values from -6 to 6
- cell_area: float32 [2, 262144], P('comp', 'rank'), may hold values from 0.5 to 2
- remap_tiles: bfloat16 [32768, 128, 128], P('rank'), may hold values from -0.5 to 0.5
- pair_blocks: int32 [64, 64], P('rank'), may hold values from 0 to 8, as said below
- slot_cell: int32 [64, 64, 8], P('rank'), may hold values from 0 to 31
- node_block: int32 [64, 512], P('rank'), may hold values from 0 to 31
Outputs:
- surface_fluxes: float32 [2, 20, 262144], P('comp', None, 'rank')
Inputs may be any that keep to these rules, and one draw needn't show every extreme that they name: `pair_blocks`: entry [q, d] counts the live slots from atmosphere rank q to ocean rank d; in some rank's row every entry is 8.
All inputs are finite; a program needn't handle non-finite values.
Results may differ from a plain program's by a relative error of at most 0.0036.
Values may be sent and summed in bfloat16 or wider, within the bound.
A program may use at most 128 MiB of HBM per device.

v0:
```python
import jax
import jax.numpy as jnp
from jax import lax
from jax.sharding import PartitionSpec as P

FLUX_IT = 5


def from_behind(value, axis, steps):
    count = lax.axis_size(axis)
    initial, last = (max(0, -steps), min(count, count - steps))
    return lax.ppermute(value, axis, [(source, source + steps) for source in range(initial, last)])


def on_device(surface_fields, cell_area, remap_tiles, pair_blocks, slot_cell, node_block):
    rank_count = lax.axis_size("rank")
    fields = surface_fields[0]
    block_width = remap_tiles.shape[1]
    slot_total = remap_tiles.shape[0]
    pair_slots = slot_cell.shape[2]
    field_rows = fields.shape[0]
    flux_rows = field_rows // 2
    nblocks = fields.shape[1] // block_width
    on_ocean = lax.axis_index("comp") == 1
    live_mask = (
        (jnp.arange(pair_slots)[None, :] < pair_blocks[0][:, None])
        .astype(jnp.float32)
        .reshape(slot_total)
    )
    block_ids = jnp.arange(nblocks, dtype=jnp.int32)
    cell_index = slot_cell[0].reshape(slot_total)
    forward_shape = (rank_count, pair_slots, field_rows, block_width)
    back_shape = (rank_count, pair_slots, flux_rows, block_width)

    def forward_products(source):
        gathered = jnp.take(source.reshape(field_rows, nblocks, block_width), node_block[0], axis=1)
        contrib = jnp.einsum(
            "fjn,jnc->jfc", gathered, remap_tiles, preferred_element_type=jnp.float32
        )
        return (contrib * live_mask[:, None, None]).astype(jnp.bfloat16).reshape(forward_shape)

    def spare_forward():
        return jnp.zeros(forward_shape, jnp.bfloat16)

    outgoing = lax.cond(on_ocean, spare_forward, lambda: forward_products(fields))
    arrived = lax.all_to_all(outgoing, "rank", split_axis=0, concat_axis=0, tiled=True)
    arrived = from_behind(arrived, "comp", 1)

    def ocean_work():
        onehot = (cell_index[None, :] == block_ids[:, None]).astype(jnp.bfloat16)
        remapped = jnp.einsum(
            "ck,kfb->cfb",
            onehot,
            arrived.reshape(slot_total, field_rows, block_width),
            preferred_element_type=jnp.float32,
        )
        surface = (
            fields.reshape(field_rows, nblocks, block_width).transpose(1, 0, 2).astype(jnp.float32)
        )
        wind_u = remapped[:, 0] - surface[:, 0]
        wind_v = remapped[:, 1] - surface[:, 1]
        wind_speed = jnp.sqrt(wind_u * wind_u + wind_v * wind_v + 0.25)
        stability = 1.0 + 4.0 * jax.nn.sigmoid(remapped[:, 2] - surface[:, 2])
        transfer = jnp.ones_like(wind_speed)
        for sweep in range(FLUX_IT):
            transfer = 1.0 / (1.0 + stability * transfer)
        fluxes = (transfer * wind_speed)[:, None, :] * (
            remapped[:, :flux_rows] - surface[:, :flux_rows]
        ) + remapped[:, flux_rows:] * surface[:, flux_rows:]
        ocean_flux = fluxes.transpose(1, 0, 2).reshape(flux_rows, nblocks * block_width)
        weighted = (fluxes * cell_area[0].reshape(nblocks, 1, block_width)).astype(jnp.bfloat16)
        sending = jnp.take(weighted, cell_index, axis=0).reshape(back_shape)
        return (ocean_flux, sending)

    def spare_ocean():
        return (
            jnp.zeros((flux_rows, nblocks * block_width), jnp.float32),
            jnp.zeros(back_shape, jnp.bfloat16),
        )

    ocean_flux, sending = lax.cond(on_ocean, ocean_work, spare_ocean)
    returned = lax.all_to_all(sending, "rank", split_axis=0, concat_axis=0, tiled=True)
    node_pick = (node_block[0][None, :] == block_ids[:, None]).astype(jnp.float32)

    def back_products(pieces):
        contrib = jnp.einsum(
            "jfc,jnc->jfn",
            pieces.reshape(slot_total, flux_rows, block_width),
            remap_tiles,
            preferred_element_type=jnp.float32,
        )
        contrib = contrib * live_mask[:, None, None]
        node_sums = jnp.einsum("kj,jfn->fkn", node_pick, contrib, precision=lax.Precision.HIGHEST)
        return node_sums.reshape(flux_rows, nblocks * block_width)

    def spare_sums():
        return jnp.zeros((flux_rows, nblocks * block_width), jnp.float32)

    handed = from_behind(returned, "comp", -1)
    node_sums = lax.cond(on_ocean, spare_sums, lambda: back_products(handed))
    atm_flux = node_sums / cell_area[0][None, :]
    return jnp.where(on_ocean, ocean_flux, atm_flux)[None]


def solution(mesh):
    return jax.shard_map(
        on_device,
        mesh=mesh,
        in_specs=(
            P("comp", None, "rank"),
            P("comp", "rank"),
            P("rank", None, None),
            P("rank", None),
            P("rank", None, None),
            P("rank", None),
        ),
        out_specs=P("comp", None, "rank"),
        check_vma=False,
    )
```

profile of v0, /device:TPU:6, one launch (start us, length us, event | category | flops | bytes accessed | tf_op | source)
XLA Modules:
  0.0 163.1 jit_solution(5913707025479758271)
XLA Ops:
  0.0 0.7 fusion.36
  0.7 18.6 %conditional.3 = (bf16[64,8,40,128]{3,2,1,0:T(8,128)(2,1)}) conditional(s32[]{:T(128)} %convert_element_type.27, (s32[1,512]{1,0:T(1,128)}, bf16[1,40,4096]{2,1,0:T(8,128)(2,1)}, bf16[512,128,128]{2,1,0:T(8,128)(2,1)}, f32[64,8]{1,0:T(8,128)S(1)}) %tuple.26, () %tuple.27), branch_computations={%region_0.1_spmd, %region_1.0_spmd} | conditional | flops 678958592 | bytes 39080968 | solution.py:45
  0.7 0.7 compare_and_fusion
  1.4 0.1 mul.54
  1.5 0.7 compare_select_fusion
  2.2 1.0 copy.29
  3.2 0.1 copy.20
  3.4 3.9 %gather_fusion.1 = bf16[512,40,128]{2,1,0:T(8,128)(2,1)} fusion(bf16[40,32,128]{2,0,1:T(8,128)(2,1)S(1)} %copy.20, s32[1024]{0:T(1024)S(1)} %pad_clamp_fusion), kind=kCustom, calls=%fused_computation | custom fusion | bytes 10487808 | tf_op jit(solution)/shard_map/cond/branch_0_fun/jit(_take)/gather | solution.py:36
  7.3 12.0 %multiply_convert_fusion = bf16[512,40,128]{2,1,0:T(8,128)(2,1)} fusion(f32[512]{0:T(512)S(1)} %mul.54, bf16[512,128,128]{2,1,0:T(8,128)(2,1)} %get-tuple-element.41, bf16[512,40,128]{2,1,0:T(8,128)(2,1)} %gather_fusion.1, pred[512]{0:T(512)(128)(4,1)S(1)} %compare_and_fusion), kind=kOutput, calls=%fused_computation.7 | convolution fusion | flops 678952960 | bytes 27265536 | tf_op jit(solution)/shard_map/cond/branch_0_fun/fjn,jnc->jfc/dot_general | solution.py:37
  19.3 3.9 %copy.22 = bf16[64,8,40,128]{3,1,2,0:T(8,128)(2,1)S(1)} copy(bf16[64,8,40,128]{3,2,1,0:T(8,128)(2,1)} %get-tuple-element.86) | data formatting | bytes 10485760 | tf_op jit(solution)/shard_map/cond | solution.py:45
  23.2 0.0 copy-start
  23.2 0.0 copy-start.1
  23.2 0.0 copy-start.3
  23.3 57.8 %all_to_all.10 = bf16[64,8,40,128]{3,1,2,0:T(8,128)(2,1)S(1)} all-to-all(bf16[64,8,40,128]{3,1,2,0:T(8,128)(2,1)S(1)} %copy.22), channel_id=1, replica_groups=mesh['comp'=2,'rank'=64] {'rank'}, dimensions={0} | all-to-all | bytes 10485760 | tf_op jit(solution)/shard_map/all_to_all | solution.py:46
  81.0 3.6 %collective-permute-start = (bf16[64,8,40,128]{3,1,2,0:T(8,128)(2,1)S(1)}, bf16[64,8,40,128]{3,1,2,0:T(8,128)(2,1)}, u32[]{:S(2)}, u32[]{:S(2)}) collective-permute-start(bf16[64,8,40,128]{3,1,2,0:T(8,128)(2,1)S(1)} %all_to_all.10), channel_id=1, source_target_pairs={{0,64},{1,65},{2,66},{3,67},{4,68},{5,69},{6,70},{7,71},{8,72},{9,... | collective-permute-start | bytes 15728648 | tf_op jit(solution)/shard_map/ppermute | solution.py:12
  84.6 6.1 %collective-permute-done = bf16[64,8,40,128]{3,1,2,0:T(8,128)(2,1)} collective-permute-done((bf16[64,8,40,128]{3,1,2,0:T(8,128)(2,1)S(1)}, bf16[64,8,40,128]{3,1,2,0:T(8,128)(2,1)}, u32[]{:S(2)}, u32[]{:S(2)}) %collective-permute-start) | collective-permute-done | bytes 5242912 | tf_op jit(solution)/shard_map/ppermute | solution.py:12
  90.7 0.0 copy-done
  90.7 0.0 copy-done.1
  90.7 0.0 copy-done.3
  90.7 3.2 %conditional.4 = (f32[20,4096]{1,0:T(8,128)}, bf16[64,8,20,128]{3,2,1,0:T(8,128)(2,1)}) conditional(s32[]{:T(128)} %convert_element_type.27, () %tuple.25, (s32[1,64,8]{1,2,0:T(8,128)S(1)}, s32[32]{0:T(128)S(1)}, bf16[64,8,40,128]{3,1,2,0:T(8,128)(2,1)}, bf16[1,40,4096]{2,1,0:T(8,128)(2,1)S(1)}, s32[1,64,8]{1,2,0:T(8,128)S(1)}, ...), branch_computations={%region_2.3_spmd, %region_3.4_spmd} | conditional | flops 169870848 | bytes 22497428 | solution.py:81
  90.7 0.8 broadcast.60
  91.5 2.4 %broadcast.61 = bf16[64,8,20,128]{3,2,1,0:T(8,128)(2,1)} broadcast(bf16[]{:T(256)} %constant.39.clone), dimensions={} | broadcast | bytes 2621442 | tf_op jit(solution)/shard_map/broadcast.4
  93.9 0.0 copy-start.2
  93.9 2.3 %copy.26 = bf16[64,8,20,128]{3,1,2,0:T(8,128)(2,1)S(1)} copy(bf16[64,8,20,128]{3,2,1,0:T(8,128)(2,1)} %get-tuple-element.56) | data formatting | bytes 5242880 | tf_op jit(solution)/shard_map/cond | solution.py:81
  96.3 37.2 %all_to_all.11 = bf16[64,8,20,128]{3,1,2,0:T(8,128)(2,1)S(1)} all-to-all(bf16[64,8,20,128]{3,1,2,0:T(8,128)(2,1)S(1)} %copy.26), channel_id=1, replica_groups=mesh['comp'=2,'rank'=64] {'rank'}, dimensions={0} | all-to-all | bytes 5242880 | tf_op jit(solution)/shard_map/all_to_all | solution.py:82
  133.4 1.3 collective-permute-start.1
  134.7 0.0 copy-done.2
  134.8 8.8 %collective-permute-done.1 = bf16[64,8,20,128]{3,1,2,0:T(8,128)(2,1)} collective-permute-done((bf16[64,8,20,128]{3,1,2,0:T(8,128)(2,1)S(1)}, bf16[64,8,20,128]{3,1,2,0:T(8,128)(2,1)}, u32[]{:S(2)}, u32[]{:S(2)}) %collective-permute-start.1) | collective-permute-done | bytes 2621472 | tf_op jit(solution)/shard_map/ppermute | solution.py:12
  143.5 18.4 %conditional.5 = (f32[20,4096]{1,0:T(8,128)S(1)}) conditional(s32[]{:T(128)} %convert_element_type.27, (bf16[64,8,20,128]{3,1,2,0:T(8,128)(2,1)}, bf16[512,128,128]{2,1,0:T(8,128)(2,1)}, f32[64,8]{1,0:T(8,128)S(1)}, f32[32,512]{1,0:T(8,128)S(1)}) %tuple.29, () %tuple.30), branch_computations={%region_4.5_spmd, %region_5.6_spmd} | conditional | flops 840171520 | bytes 37033996 | solution.py:100
  143.5 0.1 mul.72
  143.6 2.6 %copy.27 = bf16[64,8,20,128]{3,2,1,0:T(8,128)(2,1)S(1)} copy(bf16[64,8,20,128]{3,1,2,0:T(8,128)(2,1)} %get-tuple-element.76) | data formatting | bytes 5242880 | tf_op jit(solution)/shard_map
  146.2 11.8 %broadcast_multiply_fusion = f32[512,20,128]{2,1,0:T(8,128)S(1)} fusion(f32[512]{0:T(512)S(1)} %mul.72, bf16[512,20,128]{2,1,0:T(8,128)(2,1)S(1)} %bitcast.49, bf16[512,128,128]{2,1,0:T(8,128)(2,1)} %get-tuple-element.50), kind=kOutput, calls=%fused_computation.4 | convolution fusion | flops 336855040 | bytes 24643584 | tf_op jit(solution)/shard_map/cond/branch_0_fun/jfc,jnc->jfn/dot_general | solution.py:86
  158.0 3.7 %fusion.2 = f32[20,32,128]{2,1,0:T(8,128)S(1)} fusion(f32[512,20,128]{2,1,0:T(8,128)S(1)} %broadcast_multiply_fusion, f32[32,512]{1,0:T(8,128)S(1)} %get-tuple-element.52), kind=kOutput, calls=%fused_computation.5 | convolution fusion | flops 503316480 | bytes 5636096 | tf_op jit(solution)/shard_map/cond/branch_0_fun/kj,jfn->fkn/dot_general | solution.py:93
  161.7 0.2 copy.28
  162.0 0.1 divide_select_fusion
  162.0 1.1 broadcast_in_dim.31
  (4 shorter events, 0.0 us)
Async XLA Ops:
  23.2 67.5 %copy-start = (bf16[1,40,4096]{2,1,0:T(8,128)(2,1)S(1)}, bf16[1,40,4096]{2,1,0:T(8,128)(2,1)}, u32[]{:S(2)}) copy-start(bf16[1,40,4096]{2,1,0:T(8,128)(2,1)} %param.12) | copy-start | bytes 983044
  23.2 67.5 %copy-start.1 = (f32[1,4096]{1,0:T(1,128)S(1)}, f32[1,4096]{1,0:T(1,128)}, u32[]{:S(2)}) copy-start(f32[1,4096]{1,0:T(1,128)} %param.13) | copy-start | bytes 49156
  23.2 67.5 %copy-start.3 = (s32[1,64,8]{1,2,0:T(8,128)S(1)}, s32[1,64,8]{1,2,0:T(8,128)}, u32[]{:S(2)}) copy-start(s32[1,64,8]{1,2,0:T(8,128)} %param.16) | copy-start | bytes 6148
  81.0 9.7 %collective-permute-start = (bf16[64,8,40,128]{3,1,2,0:T(8,128)(2,1)S(1)}, bf16[64,8,40,128]{3,1,2,0:T(8,128)(2,1)}, u32[]{:S(2)}, u32[]{:S(2)}) collective-permute-start(bf16[64,8,40,128]{3,1,2,0:T(8,128)(2,1)S(1)} %all_to_all.10), channel_id=1, source_target_pairs={{0,64},{1,65},{2,66},{3,67},{4,68},{5,69},{6,70},{7,71},{8,72},{9,... | collective-permute-start | bytes 15728648 | tf_op jit(solution)/shard_map/ppermute | solution.py:12
  93.9 40.8 %copy-start.2 = (s32[1,512]{1,0:T(1,128)S(1)}, s32[1,512]{1,0:T(1,128)}, u32[]{:S(2)}) copy-start(s32[1,512]{1,0:T(1,128)} %param.17) | copy-start | bytes 6148
  133.4 10.1 %collective-permute-start.1 = (bf16[64,8,20,128]{3,1,2,0:T(8,128)(2,1)S(1)}, bf16[64,8,20,128]{3,1,2,0:T(8,128)(2,1)}, u32[]{:S(2)}, u32[]{:S(2)}) collective-permute-start(bf16[64,8,20,128]{3,1,2,0:T(8,128)(2,1)S(1)} %all_to_all.11), channel_id=1, source_target_pairs={{64,0},{65,1},{66,2},{67,3},{68,4},{69,5},{70,6},{71,7},{72,8},{73... | collective-permute-start | bytes 7864328 | tf_op jit(solution)/shard_map/ppermute | solution.py:12
where the time goes:
time: 166 us; the launch traced here: 163 us
  blocking collectives  94.9 us (57%)
  matrix products  27.4 us (17%)
  local copies, waits for them, and re-layouts  18.7 us (11%)
  waiting for transfers between devices  14.9 us (9%)
  starting transfers between devices  4.87 us (3%)
  other arithmetic  2.18 us (1%)
    all_to_all x1, blocking collectives, on_device(): lax.all_to_all(outgoing, 'rank', split_axis=0, concat_axis=0, tiled=True)  57.8 us
    all_to_all x1, blocking collectives, on_device(): lax.all_to_all(sending, 'rank', split_axis=0, concat_axis=0, tiled=True)  37.2 us
    ppermute x2, waiting for transfers between devices, from_behind(): lax.ppermute(value, axis, [(source, source + steps) for source in range(i...  14.9 us
    dot_general x1, matrix products, forward_products(): jnp.einsum('fjn,jnc->jfc', gathered, remap_tiles, preferred_element_type=...  12 us
    dot_general x1, matrix products, back_products(): jnp.einsum('jfc,jnc->jfn', pieces.reshape(slot_total, flux_rows, block_wi...  11.8 us
    another operation x3, local copies, waits for them, and re-layouts  5.81 us
    ppermute x2, starting transfers between devices, from_behind(): lax.ppermute(value, axis, [(source, source + steps) for source in range(i...  4.87 us
    gather x1, local copies, waits for them, and re-layouts, forward_products(): jnp.take(source.reshape(field_rows, nblocks, block_width), node_block[0],...  3.93 us
  transfers between devices with their start and end apart: 2, of which 2 were waited for; matrix products, arithmetic and copies ran while one was open for 0% of the time, Pallas kernels for 0%

commit v1 on v0

v1 whole, which is shorter than its diff:
```python
import jax
import jax.numpy as jnp
from jax import lax
from jax.experimental import pallas as pl
from jax.experimental.pallas import tpu as pltpu
from jax.sharding import PartitionSpec as P

FLUX_IT = 5
MESH = pl.DeviceIdType.MESH
F32 = jnp.float32
BF16 = jnp.bfloat16

RANKS = 64
SLOTS = 8
NCB = 32
BS = 128
F_A = 40
F_F = 20
GROUPS = F_A // 8
CHUNK = 4
NCHUNK = RANKS // CHUNK
ROWS = SLOTS * 8
BACK_ROWS = SLOTS * F_F


def offset(k):
    return (k + k // 16) % 4, (k + k // 4) % 4, k % 4


def shifted(home, k, sign):
    dy, dx, dz = offset(k)
    y, x, z = home
    if sign < 0:
        dy, dx, dz = 4 - dy, 4 - dx, 4 - dz
    return ((y + dy) % 4) * 16 + ((x + dx) % 4) * 4 + (z + dz) % 4


def shifted_lanes(home, k, sign):
    y, x, z = home
    dy, dx, dz = (k + (k >> 4)) & 3, (k + (k >> 2)) & 3, k & 3
    if sign < 0:
        dy, dx, dz = 4 - dy, 4 - dx, 4 - dz
    return ((y + dy) & 3) * 16 + ((x + dx) & 3) * 4 + ((z + dz) & 3)


def kernel(
    fields, area, tiles, nblk, pair, cell, cell_v, nblk_v, pair_v,
    out,
    tvm, blk, sbuf, rbuf, bsbuf, brbuf, pick, pick2, acc, osurf, wind, wt, stage, stage2, sums2,
    tsem, ssem, rsem, bssem, brsem,
):
    comp = lax.axis_index("comp")
    rank = lax.axis_index("rank")
    home = (rank // 16, (rank // 4) % 4, rank % 4)

    def to_ocean(k):
        return pltpu.make_async_remote_copy(
            src_ref=sbuf.at[k], dst_ref=rbuf.at[k], send_sem=ssem.at[k], recv_sem=rsem.at[k],
            device_id=(1, shifted(home, k, 1)), device_id_type=MESH,
        )

    def to_atmosphere(k):
        return pltpu.make_async_remote_copy(
            src_ref=bsbuf.at[k], dst_ref=brbuf.at[k], send_sem=bssem.at[k], recv_sem=brsem.at[k],
            device_id=(0, shifted(home, k, -1)), device_id_type=MESH,
        )

    def load_tiles(k):
        return pltpu.make_async_copy(tiles.at[shifted(home, k, 1)], tvm.at[k], tsem.at[k])

    barrier = pltpu.get_barrier_semaphore()

    def greet(k, carry):
        pl.semaphore_signal(
            barrier, inc=1, device_id=(1 - comp, shifted(home, k, 1)), device_id_type=MESH
        )
        return carry

    def permuted(b):
        columns = pl.ds(pl.multiple_of(b * BS, BS), BS)
        x = fields[:, columns].astype(F32)
        return [
            x[0:8], x[8:16], jnp.concatenate([x[16:20], x[36:40]], axis=0), x[20:28], x[28:36],
        ]

    @pl.when(comp == 0)
    def _():
        def begin(k, carry):
            load_tiles(k).start()
            return carry

        lax.fori_loop(0, RANKS, begin, 0)
        lax.fori_loop(0, RANKS, greet, 0)

        def arrange(b, carry):
            blk[b] = jnp.concatenate(permuted(b), axis=0).astype(BF16)
            return carry

        lax.fori_loop(0, NCB, arrange, 0)

        def products(k):
            d = shifted(home, k, 1)
            load_tiles(k).wait()
            live = pair[0, d]
            for s in range(0, SLOTS, 2):
                both = []
                for e in (s, s + 1):
                    lhs = blk[nblk[0, d * SLOTS + e]]
                    r = jnp.dot(lhs, tvm[k, e], preferred_element_type=F32)
                    both.append(r * (e < live).astype(F32))
                for g in range(GROUPS):
                    rows = slice(g * 8, g * 8 + 8)
                    sbuf[k, g, s * 8 : s * 8 + 16, :] = jnp.concatenate(
                        [both[0][rows], both[1][rows]], axis=0
                    ).astype(BF16)

        AHEAD = 4
        for k in range(AHEAD):
            products(k)
        pl.semaphore_wait(barrier, RANKS)
        for k in range(AHEAD):
            to_ocean(k).start()

        def step(k, carry):
            products(k)
            to_ocean(k).start()
            return carry

        lax.fori_loop(AHEAD, RANKS, step, 0)

        def build(i, carry):
            lane = lax.broadcasted_iota(jnp.int32, (1, 256), 1)
            kk = i * CHUNK + (lane >> 6)
            where_k = shifted_lanes(home, kk, 1)
            slot = (lane >> 3) & 7
            q = lax.broadcasted_iota(jnp.int32, (RANKS, 256), 0)
            j = lax.broadcasted_iota(jnp.int32, (RANKS * SLOTS, 256), 0)
            ej = (j == where_k * SLOTS + slot).astype(F32).astype(BF16)
            ed = (q == where_k).astype(F32).astype(BF16)
            nb = jnp.broadcast_to(nblk_v[...].astype(F32), (8, RANKS * SLOTS)).astype(BF16)
            pb = jnp.broadcast_to(pair_v[...].astype(F32), (8, RANKS)).astype(BF16)
            block = jnp.dot(nb, ej, preferred_element_type=F32)[0:1]
            count = jnp.dot(pb, ed, preferred_element_type=F32)[0:1]
            block = jnp.where(slot.astype(F32) < count, block, 100.0)
            key = block * 8.0 + (lane & 7).astype(F32)
            row = lax.broadcasted_iota(jnp.int32, (256, 256), 0).astype(F32)
            pick[i] = (row == key).astype(F32).astype(BF16)
            lane = lax.broadcasted_iota(jnp.int32, (1, 128), 1)
            kk = i * CHUNK + (lane >> 5)
            where_k = shifted_lanes(home, kk, 1)
            slot = (lane >> 2) & 7
            q = lax.broadcasted_iota(jnp.int32, (RANKS, 128), 0)
            j = lax.broadcasted_iota(jnp.int32, (RANKS * SLOTS, 128), 0)
            ej = (j == where_k * SLOTS + slot).astype(F32).astype(BF16)
            ed = (q == where_k).astype(F32).astype(BF16)
            block = jnp.dot(nb, ej, preferred_element_type=F32)[0:1]
            count = jnp.dot(pb, ed, preferred_element_type=F32)[0:1]
            block = jnp.where(slot.astype(F32) < count, block, 100.0)
            key = block * 4.0 + (lane & 3).astype(F32)
            row = lax.broadcasted_iota(jnp.int32, (128, 128), 0).astype(F32)
            pick2[i] = (row == key).astype(F32).astype(BF16)
            return carry

        lax.fori_loop(0, NCHUNK, build, 0)
        acc[...] = jnp.zeros_like(acc)
        sums2[...] = jnp.zeros_like(sums2)

        def split(r):
            hi = r.astype(BF16)
            return jnp.concatenate([hi, (r - hi.astype(F32)).astype(BF16)], axis=1)

        def back(i, carry):
            for c in range(CHUNK):
                k = i * CHUNK + c
                to_atmosphere(k).wait_recv()
                for p in range(SLOTS // 2):
                    lhs = jnp.concatenate(
                        [
                            brbuf[k, p * 16 : p * 16 + 16],
                            brbuf[k, 64 + p * 16 : 64 + p * 16 + 16],
                            brbuf[k, 128 + p * 8 : 128 + p * 8 + 8],
                        ],
                        axis=0,
                    )
                    rhs = tvm[k, 2 * p : 2 * p + 2].reshape(2 * BS, BS)
                    r = lax.dot_general(
                        lhs, rhs, (((1,), (1,)), ((), ())), preferred_element_type=F32
                    )
                    low, high = r[:, :BS], r[:, BS:]
                    rows = slice(c * 64 + p * 16, c * 64 + p * 16 + 16)
                    stage[0, rows] = split(jnp.concatenate([low[0:8], high[8:16]], axis=0))
                    stage[1, rows] = split(jnp.concatenate([low[16:24], high[24:32]], axis=0))
                    sub = lax.broadcasted_iota(jnp.int32, (8, BS), 0)
                    last = jnp.where(sub < 4, low[32:40], high[32:40])
                    rows = slice(c * 32 + p * 8, c * 32 + p * 8 + 8)
                    stage2[rows] = split(last)
            for g in (0, 1):
                r = jnp.dot(pick[i], stage[g], preferred_element_type=F32)
                acc[g] += r[:, :BS] + r[:, BS:]
            r = jnp.dot(pick2[i], stage2[...], preferred_element_type=F32)
            sums2[...] += r[:, :BS] + r[:, BS:]
            return carry

        lax.fori_loop(0, NCHUNK, back, 0)

        for b in range(NCB):
            a = area[0:1, b * BS : (b + 1) * BS]
            out[0:8, b * BS : (b + 1) * BS] = acc[0, b * 8 : b * 8 + 8] / a
            out[8:16, b * BS : (b + 1) * BS] = acc[1, b * 8 : b * 8 + 8] / a
            out[16:20, b * BS : (b + 1) * BS] = sums2[b * 4 : b * 4 + 4] / a

        def sent(k, carry):
            to_ocean(k).wait_send()
            return carry

        lax.fori_loop(0, RANKS, sent, 0)

    @pl.when(comp == 1)
    def _():
        lax.fori_loop(0, RANKS, greet, 0)

        def arrange(b, carry):
            rows = pl.ds(pl.multiple_of(b * 8, 8), 8)
            for g, part in enumerate(permuted(b)):
                osurf[g, rows] = part
            return carry

        lax.fori_loop(0, NCB, arrange, 0)

        def build(i, carry):
            lane = lax.broadcasted_iota(jnp.int32, (1, 256), 1)
            kk = i * CHUNK + (lane >> 6)
            where_k = shifted_lanes(home, kk, -1)
            slot = (lane >> 3) & 7
            q = lax.broadcasted_iota(jnp.int32, (RANKS, 256), 0)
            ed = (q == where_k).astype(F32).astype(BF16)
            cells = jnp.dot(cell_v[...].astype(F32).astype(BF16), ed, preferred_element_type=F32)
            s = lax.broadcasted_iota(jnp.int32, (SLOTS, 256), 0)
            mine = jnp.sum(jnp.where(s == slot, cells, 0.0), axis=0, keepdims=True)
            key = mine * 8.0 + (lane & 7).astype(F32)
            row = lax.broadcasted_iota(jnp.int32, (256, 256), 0).astype(F32)
            pick[i] = (row == key).astype(F32).astype(BF16)
            return carry

        lax.fori_loop(0, NCHUNK, build, 0)
        acc[...] = jnp.zeros_like(acc)
        pl.semaphore_wait(barrier, RANKS)

        def reduce(i, carry):
            for c in range(CHUNK):
                to_ocean(i * CHUNK + c).wait_recv()
            for g in range(GROUPS):
                rhs = rbuf[pl.ds(i * CHUNK, CHUNK), g].reshape(CHUNK * ROWS, BS)
                acc[g] += jnp.dot(pick[i], rhs, preferred_element_type=F32)
            return carry

        lax.fori_loop(0, NCHUNK, reduce, 0)

        def difference(f):
            rows = pl.ds(f, NCB, stride=8)
            return acc[0, rows, :] - osurf[0, rows, :]

        wind_u = difference(0)
        wind_v = difference(1)
        wind_speed = jnp.sqrt(wind_u * wind_u + wind_v * wind_v + 0.25)
        stability = 1.0 + 4.0 * jax.nn.sigmoid(difference(2))
        transfer = jnp.ones_like(wind_speed)
        for sweep in range(FLUX_IT):
            transfer = 1.0 / (1.0 + stability * transfer)
        wind[...] = transfer * wind_speed

        for c in range(NCB):
            rows = slice(c * 8, c * 8 + 8)
            columns = slice(c * BS, (c + 1) * BS)
            scale = jnp.broadcast_to(wind[c : c + 1], (8, BS))
            a = jnp.broadcast_to(area[0:1, columns], (8, BS))
            x = [acc[g, rows] for g in range(GROUPS)]
            o = [osurf[g, rows] for g in range(GROUPS)]
            first = scale * (x[0] - o[0]) + x[3] * o[3]
            second = scale * (x[1] - o[1]) + x[4] * o[4]
            third = scale * (x[2] - o[2]) + pltpu.roll(x[2] * o[2], 4, 0)
            out[0:8, columns] = first
            out[8:16, columns] = second
            out[16:20, columns] = third[0:4]
            sub = lax.broadcasted_iota(jnp.int32, (8, BS), 0)
            third = jnp.where(sub < 4, third * a, 0.0).astype(BF16).astype(F32)
            wt[c, 0] = (first * a).astype(BF16).astype(F32)
            wt[c, 1] = (second * a).astype(BF16).astype(F32)
            wt[c, 2] = third
            wt[c, 3] = pltpu.roll(third, 4, 0)

        def send_back(k, carry):
            q = shifted(home, k, -1)
            cells = [cell[s, q] for s in range(SLOTS)]
            for g in (0, 1):
                for s in range(0, SLOTS, 2):
                    bsbuf[k, g * 64 + s * 8 : g * 64 + s * 8 + 16] = jnp.concatenate(
                        [wt[cells[s], g], wt[cells[s + 1], g]], axis=0
                    ).astype(BF16)
            for s in range(0, SLOTS, 4):
                bsbuf[k, 128 + s * 4 : 128 + s * 4 + 16] = jnp.concatenate(
                    [
                        wt[cells[s], 2] + wt[cells[s + 1], 3],
                        wt[cells[s + 2], 2] + wt[cells[s + 3], 3],
                    ],
                    axis=0,
                ).astype(BF16)
            to_atmosphere(k).start()
            return carry

        lax.fori_loop(0, RANKS, send_back, 0)

        def sent(k, carry):
            to_atmosphere(k).wait_send()
            return carry

        lax.fori_loop(0, RANKS, sent, 0)


def on_device(surface_fields, cell_area, remap_tiles, pair_blocks, slot_cell, node_block):
    vmem = pl.BlockSpec(memory_space=pltpu.VMEM)
    smem = pl.BlockSpec(memory_space=pltpu.SMEM)
    cells = slot_cell[0].T
    out = pl.pallas_call(
        kernel,
        out_shape=jax.ShapeDtypeStruct((F_F, NCB * BS), F32),
        in_specs=[vmem, vmem, pl.BlockSpec(memory_space=pl.ANY), smem, smem, smem, vmem, vmem, vmem],
        out_specs=vmem,
        scratch_shapes=[
            pltpu.VMEM((RANKS, SLOTS, BS, BS), BF16),
            pltpu.VMEM((NCB, F_A, BS), BF16),
            pltpu.VMEM((RANKS, GROUPS, ROWS, BS), BF16),
            pltpu.VMEM((RANKS, GROUPS, ROWS, BS), BF16),
            pltpu.VMEM((RANKS, BACK_ROWS, BS), BF16),
            pltpu.VMEM((RANKS, BACK_ROWS, BS), BF16),
            pltpu.VMEM((NCHUNK, 256, 256), BF16),
            pltpu.VMEM((NCHUNK, 128, 128), BF16),
            pltpu.VMEM((GROUPS, NCB * 8, BS), F32),
            pltpu.VMEM((GROUPS, NCB * 8, BS), F32),
            pltpu.VMEM((NCB, BS), F32),
            pltpu.VMEM((NCB, 4, 8, BS), F32),
            pltpu.VMEM((2, 256, 2 * BS), BF16),
            pltpu.VMEM((128, 2 * BS), BF16),
            pltpu.VMEM((NCB * 4, BS), F32),
            pltpu.SemaphoreType.DMA((RANKS,)),
            pltpu.SemaphoreType.DMA((RANKS,)),
            pltpu.SemaphoreType.DMA((RANKS,)),
            pltpu.SemaphoreType.DMA((RANKS,)),
            pltpu.SemaphoreType.DMA((RANKS,)),
        ],
        compiler_params=pltpu.CompilerParams(
            collective_id=0, has_side_effects=True, vmem_limit_bytes=56 << 20
        ),
    )(
        surface_fields[0], cell_area, remap_tiles.reshape(RANKS, SLOTS, BS, BS),
        node_block, pair_blocks, cells, cells, node_block, pair_blocks,
    )
    return out[None]


def solution(mesh):
    return jax.shard_map(
        on_device,
        mesh=mesh,
        in_specs=(
            P("comp", None, "rank"),
            P("comp", "rank"),
            P("rank", None, None),
            P("rank", None),
            P("rank", None, None),
            P("rank", None),
        ),
        out_specs=P("comp", None, "rank"),
        check_vma=False,
    )
```

time: 166 us -> 78.1 us (0.47); the launches traced: 163 us -> 77.9 us
  blocking collectives: 94.9 us -> 0 us
  Pallas kernels: 0 us -> 75.8 us
  matrix products: 27.4 us -> 0 us
  local copies, waits for them, and re-layouts: 18.7 us -> 2.06 us
  waiting for transfers between devices: 14.9 us -> 0 us
  starting transfers between devices: 4.87 us -> 0 us
  other arithmetic: 2.18 us -> 0 us
    all_to_all x2 -> x0, blocking collectives: 94.9 us -> none  [the longest x1 57.8 us: on_device(): lax.all_to_all(outgoing, 'rank', split_axis=0, concat_axis=0, tiled=True)]
    pallas_call x0 -> x1, Pallas kernels: none -> 75.8 us  [on_device(): pl.pallas_call(kernel, out_shape=jax.ShapeDtypeStruct((F_F, NCB * BS), F3...]
    dot_general x3 -> x0, matrix products: 27.4 us -> none  [the longest x1 12 us: forward_products(): jnp.einsum('fjn,jnc->jfc', gathered, remap_tiles, preferred_element_type=...]
    ppermute x2 -> x0, waiting for transfers between devices: 14.9 us -> none  [from_behind(): lax.ppermute(value, axis, [(source, source + steps) for source in range(i...]
    cond x5 -> x0, local copies, waits for them, and re-layouts: 7.52 us -> none  [the longest x1 3.92 us: on_device(): lax.cond(on_ocean, spare_forward, lambda: forward_products(fields))]
    another operation x4 -> x0, local copies, waits for them, and re-layouts: 5.94 us -> none
    ppermute x2 -> x0, starting transfers between devices: 4.87 us -> none  [from_behind(): lax.ppermute(value, axis, [(source, source + steps) for source in range(i...]
    gather x1 -> x0, local copies, waits for them, and re-layouts: 3.93 us -> none  [forward_products(): jnp.take(source.reshape(field_rows, nblocks, block_width), node_block[0],...]
  transfers between devices with their start and end apart: 2 -> 0, of which waited for: 2 -> 0; matrix products, arithmetic and copies ran while one was open for 0% -> 0% of each run, Pallas kernels for 0% -> 0%
where the time goes in v1:
time: 78.1 us; the launch traced here: 77.9 us
  Pallas kernels  75.8 us (97%)
  local copies, waits for them, and re-layouts  2.06 us (3%)
    pallas_call x1, Pallas kernels, on_device(): pl.pallas_call(kernel, out_shape=jax.ShapeDtypeStruct((F_F, NCB * BS), F3...  75.8 us
    broadcast_in_dim x1, local copies, waits for them, and re-layouts, on_device(): return out[None]  2.06 us

profile of v1, /device:TPU:6, one launch (start us, length us, event | category | flops | bytes accessed | tf_op | source)
XLA Modules:
  0.0 77.9 jit_solution(5616591390637278742)
XLA Ops:
  0.0 75.8 %shard_map.64 = f32[20,4096]{1,0:T(8,128)} custom-call(bf16[40,4096]{1,0:T(8,128)(2,1)} %bitcast.8, f32[1,4096]{1,0:T(1,128)} %area.1, bf16[64,8,128,128]{3,2,1,0:T(8,128)(2,1)} %bitcast.6, s32[1,512]{1,0:T(1,128)} %nblk_v.1, s32[1,64]{1,0:T(1,128)} %pair_v.1, s32[8,64]{1,0:T(8,128)} %bitcast.9, s32[8,64]{1,0:T(8,128)} %bitcast.10, s32[1,512]{1,0:T(1,128)} %nblk_v.1, ...), custom_call_target="tpu_custom_call" | custom-call | tf_op jit(solution)/shard_map/pallas_call | solution.py:324
  75.9 2.1 %copy.7 = f32[1,20,4096]{2,0,1:T(1,128)} copy(f32[1,20,4096]{2,1,0:T(8,128)} %bitcast.7) | data formatting | bytes 655360 | tf_op jit(solution)/shard_map/broadcast_in_dim | solution.py:358

commit v2 on v1

--- a/solution.py
+++ b/solution.py
@@ -24,7 +24,7 @@
 
 
 def offset(k):
-    return (k + k // 16) % 4, (k + k // 4) % 4, k % 4
+    return (k + (k >> 4)) & 3, (k + (k >> 2)) & 3, k & 3
 
 
 def shifted(home, k, sign):
@@ -32,15 +32,7 @@
     y, x, z = home
     if sign < 0:
         dy, dx, dz = 4 - dy, 4 - dx, 4 - dz
-    return ((y + dy) % 4) * 16 + ((x + dx) % 4) * 4 + (z + dz) % 4
-
-
-def shifted_lanes(home, k, sign):
-    y, x, z = home
-    dy, dx, dz = (k + (k >> 4)) & 3, (k + (k >> 2)) & 3, k & 3
-    if sign < 0:
-        dy, dx, dz = 4 - dy, 4 - dx, 4 - dz
-    return ((y + dy) & 3) * 16 + ((x + dx) & 3) * 4 + ((z + dz) & 3)
+    return (((y + dy) & 3) << 4) + (((x + dx) & 3) << 2) + ((z + dz) & 3)
 
 
 def kernel(
@@ -51,7 +43,7 @@
 ):
     comp = lax.axis_index("comp")
     rank = lax.axis_index("rank")
-    home = (rank // 16, (rank // 4) % 4, rank % 4)
+    home = (rank >> 4, (rank >> 2) & 3, rank & 3)
 
     def to_ocean(k):
         return pltpu.make_async_remote_copy(
@@ -72,9 +64,11 @@
 
     def greet(k, carry):
         pl.semaphore_signal(
-            barrier, inc=1, device_id=(1 - comp, shifted(home, k, 1)), device_id_type=MESH
+            barrier, inc=1, device_id=(1 - comp, (rank + k) & (RANKS - 1)), device_id_type=MESH
         )
         return carry
+
+    lax.fori_loop(0, RANKS, greet, 0)
 
     def permuted(b):
         columns = pl.ds(pl.multiple_of(b * BS, BS), BS)
@@ -90,7 +84,6 @@
             return carry
 
         lax.fori_loop(0, RANKS, begin, 0)
-        lax.fori_loop(0, RANKS, greet, 0)
 
         def arrange(b, carry):
             blk[b] = jnp.concatenate(permuted(b), axis=0).astype(BF16)
@@ -115,23 +108,28 @@
                     ).astype(BF16)
 
         AHEAD = 4
-        for k in range(AHEAD):
+        def ahead(k, carry):
             products(k)
-        pl.semaphore_wait(barrier, RANKS)
-        for k in range(AHEAD):
+            return carry
+
+        def release(k, carry):
             to_ocean(k).start()
+            return carry
 
         def step(k, carry):
             products(k)
             to_ocean(k).start()
             return carry
 
+        lax.fori_loop(0, AHEAD, ahead, 0)
+        pl.semaphore_wait(barrier, RANKS)
+        lax.fori_loop(0, AHEAD, release, 0)
         lax.fori_loop(AHEAD, RANKS, step, 0)
 
         def build(i, carry):
             lane = lax.broadcasted_iota(jnp.int32, (1, 256), 1)
             kk = i * CHUNK + (lane >> 6)
-            where_k = shifted_lanes(home, kk, 1)
+            where_k = shifted(home, kk, 1)
             slot = (lane >> 3) & 7
             q = lax.broadcasted_iota(jnp.int32, (RANKS, 256), 0)
             j = lax.broadcasted_iota(jnp.int32, (RANKS * SLOTS, 256), 0)
@@ -147,7 +145,7 @@
             pick[i] = (row == key).astype(F32).astype(BF16)
             lane = lax.broadcasted_iota(jnp.int32, (1, 128), 1)
             kk = i * CHUNK + (lane >> 5)
-            where_k = shifted_lanes(home, kk, 1)
+            where_k = shifted(home, kk, 1)
             slot = (lane >> 2) & 7
             q = lax.broadcasted_iota(jnp.int32, (RANKS, 128), 0)
             j = lax.broadcasted_iota(jnp.int32, (RANKS * SLOTS, 128), 0)
@@ -169,10 +167,16 @@
             hi = r.astype(BF16)
             return jnp.concatenate([hi, (r - hi.astype(F32)).astype(BF16)], axis=1)
 
-        def back(i, carry):
+        def collect(i, half):
+            for g in (0, 1):
+                r = jnp.dot(pick[i], stage[half, g], preferred_element_type=F32)
+                acc[g] += r[:, :BS] + r[:, BS:]
+            r = jnp.dot(pick2[i], stage2[half], preferred_element_type=F32)
+            sums2[...] += r[:, :BS] + r[:, BS:]
+
+        def back_products(i, half):
             for c in range(CHUNK):
                 k = i * CHUNK + c
-                to_atmosphere(k).wait_recv()
                 for p in range(SLOTS // 2):
                     lhs = jnp.concatenate(
                         [
@@ -188,20 +192,33 @@
                     )
                     low, high = r[:, :BS], r[:, BS:]
                     rows = slice(c * 64 + p * 16, c * 64 + p * 16 + 16)
-                    stage[0, rows] = split(jnp.concatenate([low[0:8], high[8:16]], axis=0))
-                    stage[1, rows] = split(jnp.concatenate([low[16:24], high[24:32]], axis=0))
+                    stage[half, 0, rows] = split(jnp.concatenate([low[0:8], high[8:16]], axis=0))
+                    stage[half, 1, rows] = split(jnp.concatenate([low[16:24], high[24:32]], axis=0))
                     sub = lax.broadcasted_iota(jnp.int32, (8, BS), 0)
                     last = jnp.where(sub < 4, low[32:40], high[32:40])
                     rows = slice(c * 32 + p * 8, c * 32 + p * 8 + 8)
-                    stage2[rows] = split(last)
-            for g in (0, 1):
-                r = jnp.dot(pick[i], stage[g], preferred_element_type=F32)
-                acc[g] += r[:, :BS] + r[:, BS:]
-            r = jnp.dot(pick2[i], stage2[...], preferred_element_type=F32)
-            sums2[...] += r[:, :BS] + r[:, BS:]
-            return carry
-
-        lax.fori_loop(0, NCHUNK, back, 0)
+                    stage2[half, rows] = split(last)
+
+        def arrived(i):
+            for c in range(CHUNK):
+                to_atmosphere(i * CHUNK + c).wait_recv()
+
+        arrived(0)
+        back_products(0, 0)
+
+        def back(m, carry):
+            for e in range(2):
+                i = 2 * m + 1 + e
+                arrived(i)
+                collect(i - 1, e)
+                back_products(i, 1 - e)
+            return carry
+
+        lax.fori_loop(0, (NCHUNK - 2) // 2, back, 0)
+        arrived(NCHUNK - 1)
+        collect(NCHUNK - 2, 0)
+        back_products(NCHUNK - 1, 1)
+        collect(NCHUNK - 1, 1)
 
         for b in range(NCB):
             a = area[0:1, b * BS : (b + 1) * BS]
@@ -217,8 +234,6 @@
 
     @pl.when(comp == 1)
     def _():
-        lax.fori_loop(0, RANKS, greet, 0)
-
         def arrange(b, carry):
             rows = pl.ds(pl.multiple_of(b * 8, 8), 8)
             for g, part in enumerate(permuted(b)):
@@ -230,7 +245,7 @@
         def build(i, carry):
             lane = lax.broadcasted_iota(jnp.int32, (1, 256), 1)
             kk = i * CHUNK + (lane >> 6)
-            where_k = shifted_lanes(home, kk, -1)
+            where_k = shifted(home, kk, -1)
             slot = (lane >> 3) & 7
             q = lax.broadcasted_iota(jnp.int32, (RANKS, 256), 0)
             ed = (q == where_k).astype(F32).astype(BF16)
@@ -339,8 +354,8 @@
             pltpu.VMEM((GROUPS, NCB * 8, BS), F32),
             pltpu.VMEM((NCB, BS), F32),
             pltpu.VMEM((NCB, 4, 8, BS), F32),
-            pltpu.VMEM((2, 256, 2 * BS), BF16),
-            pltpu.VMEM((128, 2 * BS), BF16),
+            pltpu.VMEM((2, 2, 256, 2 * BS), BF16),
+            pltpu.VMEM((2, 128, 2 * BS), BF16),
             pltpu.VMEM((NCB * 4, BS), F32),
             pltpu.SemaphoreType.DMA((RANKS,)),
             pltpu.SemaphoreType.DMA((RANKS,)),

time: 78.1 us -> 70.5 us (0.903); the launches traced: 77.9 us -> 69.2 us
  Pallas kernels: 75.8 us -> 67.1 us
    pallas_call x1, Pallas kernels: 75.8 us -> 67.1 us  [on_device(): pl.pallas_call(kernel, out_shape=jax.ShapeDtypeStruct((F_F, NCB * BS), F3...]
where the time goes in v2:
time: 70.5 us; the launch traced here: 69.2 us
  Pallas kernels  67.1 us (95%)
  local copies, waits for them, and re-layouts  2.06 us (3%)
    pallas_call x1, Pallas kernels, on_device(): pl.pallas_call(kernel, out_shape=jax.ShapeDtypeStruct((F_F, NCB * BS), F3...  67.1 us
    broadcast_in_dim x1, local copies, waits for them, and re-layouts, on_device(): return out[None]  2.06 us

profile of v2, /device:TPU:6, one launch (start us, length us, event | category | flops | bytes accessed | tf_op | source)
XLA Modules:
  0.0 69.2 jit_solution(3027160402443122846)
XLA Ops:
  0.0 67.1 %shard_map.64 = f32[20,4096]{1,0:T(8,128)} custom-call(bf16[40,4096]{1,0:T(8,128)(2,1)} %bitcast.8, f32[1,4096]{1,0:T(1,128)} %area.1, bf16[64,8,128,128]{3,2,1,0:T(8,128)(2,1)} %bitcast.6, s32[1,512]{1,0:T(1,128)} %nblk_v.1, s32[1,64]{1,0:T(1,128)} %pair_v.1, s32[8,64]{1,0:T(8,128)} %bitcast.9, s32[8,64]{1,0:T(8,128)} %bitcast.10, s32[1,512]{1,0:T(1,128)} %nblk_v.1, ...), custom_call_target="tpu_custom_call" | custom-call | tf_op jit(solution)/shard_map/pallas_call | solution.py:339
  67.1 2.1 %copy.7 = f32[1,20,4096]{2,0,1:T(1,128)} copy(f32[1,20,4096]{2,1,0:T(8,128)} %bitcast.7) | data formatting | bytes 655360 | tf_op jit(solution)/shard_map/broadcast_in_dim | solution.py:373

commit v3 on v2

--- a/solution.py
+++ b/solution.py
@@ -24,7 +24,8 @@
 
 
 def offset(k):
-    return (k + (k >> 4)) & 3, (k + (k >> 2)) & 3, k & 3
+    o = ((k + 1) * 27) & 63
+    return o >> 4, (o >> 2) & 3, o & 3
 
 
 def shifted(home, k, sign):
@@ -36,10 +37,10 @@
 
 
 def kernel(
-    fields, area, tiles, nblk, pair, cell, cell_v, nblk_v, pair_v,
+    fields_hbm, area_hbm, tiles, nblk_hbm, pair_hbm, cell_hbm,
     out,
     tvm, blk, sbuf, rbuf, bsbuf, brbuf, pick, pick2, acc, osurf, wind, wt, stage, stage2, sums2,
-    tsem, ssem, rsem, bssem, brsem,
+    fields, area, nblk, pair, cell, nblk_v, pair_v, cell_v, tsem, ssem, rsem, bssem, brsem, isem,
 ):
     comp = lax.axis_index("comp")
     rank = lax.axis_index("rank")
@@ -47,13 +48,13 @@
 
     def to_ocean(k):
         return pltpu.make_async_remote_copy(
-            src_ref=sbuf.at[k], dst_ref=rbuf.at[k], send_sem=ssem.at[k], recv_sem=rsem.at[k],
+            src_ref=sbuf.at[k], dst_ref=rbuf.at[k], send_sem=ssem, recv_sem=rsem.at[k],
             device_id=(1, shifted(home, k, 1)), device_id_type=MESH,
         )
 
     def to_atmosphere(k):
         return pltpu.make_async_remote_copy(
-            src_ref=bsbuf.at[k], dst_ref=brbuf.at[k], send_sem=bssem.at[k], recv_sem=brsem.at[k],
+            src_ref=bsbuf.at[k], dst_ref=brbuf.at[k], send_sem=bssem, recv_sem=brsem.at[k],
             device_id=(0, shifted(home, k, -1)), device_id_type=MESH,
         )
 
@@ -64,11 +65,22 @@
 
     def greet(k, carry):
         pl.semaphore_signal(
-            barrier, inc=1, device_id=(1 - comp, (rank + k) & (RANKS - 1)), device_id_type=MESH
+            barrier, inc=1, device_id=(1 - comp, (rank + 42 + jnp.where((k & 1) == 0, k >> 1, -((k + 1) >> 1))) & (RANKS - 1)), device_id_type=MESH
         )
         return carry
 
     lax.fori_loop(0, RANKS, greet, 0)
+    loads = [
+        pltpu.make_async_copy(source, target, isem.at[n])
+        for n, (source, target) in enumerate(
+            (
+                (fields_hbm, fields), (nblk_hbm, nblk), (pair_hbm, pair), (cell_hbm, cell),
+                (nblk_hbm, nblk_v), (pair_hbm, pair_v), (cell_hbm, cell_v), (area_hbm, area),
+            )
+        )
+    ]
+    for load in loads:
+        load.start()
 
     def permuted(b):
         columns = pl.ds(pl.multiple_of(b * BS, BS), BS)
@@ -84,6 +96,8 @@
             return carry
 
         lax.fori_loop(0, RANKS, begin, 0)
+        for load in loads:
+            load.wait()
 
         def arrange(b, carry):
             blk[b] = jnp.concatenate(permuted(b), axis=0).astype(BF16)
@@ -107,7 +121,7 @@
                         [both[0][rows], both[1][rows]], axis=0
                     ).astype(BF16)
 
-        AHEAD = 4
+        AHEAD = 6
         def ahead(k, carry):
             products(k)
             return carry
@@ -161,6 +175,7 @@
 
         lax.fori_loop(0, NCHUNK, build, 0)
         acc[...] = jnp.zeros_like(acc)
+        area[...] = 1.0 / area[...]
         sums2[...] = jnp.zeros_like(sums2)
 
         def split(r):
@@ -204,6 +219,7 @@
                 to_atmosphere(i * CHUNK + c).wait_recv()
 
         arrived(0)
+        pltpu.make_async_copy(sbuf, sbuf, ssem).wait()
         back_products(0, 0)
 
         def back(m, carry):
@@ -221,19 +237,17 @@
         collect(NCHUNK - 1, 1)
 
         for b in range(NCB):
-            a = area[0:1, b * BS : (b + 1) * BS]
-            out[0:8, b * BS : (b + 1) * BS] = acc[0, b * 8 : b * 8 + 8] / a
-            out[8:16, b * BS : (b + 1) * BS] = acc[1, b * 8 : b * 8 + 8] / a
-            out[16:20, b * BS : (b + 1) * BS] = sums2[b * 4 : b * 4 + 4] / a
-
-        def sent(k, carry):
-            to_ocean(k).wait_send()
-            return carry
-
-        lax.fori_loop(0, RANKS, sent, 0)
+            columns = slice(b * BS, (b + 1) * BS)
+            scale = area[0:1, columns]
+            out[0:8, 0, columns] = acc[0, b * 8 : b * 8 + 8] * scale
+            out[8:16, 0, columns] = acc[1, b * 8 : b * 8 + 8] * scale
+            out[16:20, 0, columns] = sums2[b * 4 : b * 4 + 4] * scale
 
     @pl.when(comp == 1)
     def _():
+        for load in loads:
+            load.wait()
+
         def arrange(b, carry):
             rows = pl.ds(pl.multiple_of(b * 8, 8), 8)
             for g, part in enumerate(permuted(b)):
@@ -264,9 +278,11 @@
         def reduce(i, carry):
             for c in range(CHUNK):
                 to_ocean(i * CHUNK + c).wait_recv()
-            for g in range(GROUPS):
-                rhs = rbuf[pl.ds(i * CHUNK, CHUNK), g].reshape(CHUNK * ROWS, BS)
-                acc[g] += jnp.dot(pick[i], rhs, preferred_element_type=F32)
+            for groups in ((0, 1), (2, 3), (4,)):
+                rhs = [rbuf[pl.ds(i * CHUNK, CHUNK), g].reshape(CHUNK * ROWS, BS) for g in groups]
+                r = jnp.dot(pick[i], jnp.concatenate(rhs, axis=1), preferred_element_type=F32)
+                for n, g in enumerate(groups):
+                    acc[g] += r[:, n * BS : (n + 1) * BS]
             return carry
 
         lax.fori_loop(0, NCHUNK, reduce, 0)
@@ -294,9 +310,9 @@
             first = scale * (x[0] - o[0]) + x[3] * o[3]
             second = scale * (x[1] - o[1]) + x[4] * o[4]
             third = scale * (x[2] - o[2]) + pltpu.roll(x[2] * o[2], 4, 0)
-            out[0:8, columns] = first
-            out[8:16, columns] = second
-            out[16:20, columns] = third[0:4]
+            out[0:8, 0, columns] = first
+            out[8:16, 0, columns] = second
+            out[16:20, 0, columns] = third[0:4]
             sub = lax.broadcasted_iota(jnp.int32, (8, BS), 0)
             third = jnp.where(sub < 4, third * a, 0.0).astype(BF16).astype(F32)
             wt[c, 0] = (first * a).astype(BF16).astype(F32)
@@ -325,21 +341,16 @@
 
         lax.fori_loop(0, RANKS, send_back, 0)
 
-        def sent(k, carry):
-            to_atmosphere(k).wait_send()
-            return carry
-
-        lax.fori_loop(0, RANKS, sent, 0)
+        pltpu.make_async_copy(bsbuf, bsbuf, bssem).wait()
 
 
 def on_device(surface_fields, cell_area, remap_tiles, pair_blocks, slot_cell, node_block):
     vmem = pl.BlockSpec(memory_space=pltpu.VMEM)
-    smem = pl.BlockSpec(memory_space=pltpu.SMEM)
-    cells = slot_cell[0].T
+    hbm = pl.BlockSpec(memory_space=pl.ANY)
     out = pl.pallas_call(
         kernel,
-        out_shape=jax.ShapeDtypeStruct((F_F, NCB * BS), F32),
-        in_specs=[vmem, vmem, pl.BlockSpec(memory_space=pl.ANY), smem, smem, smem, vmem, vmem, vmem],
+        out_shape=jax.ShapeDtypeStruct((F_F, 1, NCB * BS), F32),
+        in_specs=[hbm] * 6,
         out_specs=vmem,
         scratch_shapes=[
             pltpu.VMEM((RANKS, SLOTS, BS, BS), BF16),
@@ -357,20 +368,29 @@
             pltpu.VMEM((2, 2, 256, 2 * BS), BF16),
             pltpu.VMEM((2, 128, 2 * BS), BF16),
             pltpu.VMEM((NCB * 4, BS), F32),
+            pltpu.VMEM((F_A, NCB * BS), BF16),
+            pltpu.VMEM((1, NCB * BS), F32),
+            pltpu.SMEM((1, RANKS * SLOTS), jnp.int32),
+            pltpu.SMEM((1, RANKS), jnp.int32),
+            pltpu.SMEM((SLOTS, RANKS), jnp.int32),
+            pltpu.VMEM((1, RANKS * SLOTS), jnp.int32),
+            pltpu.VMEM((1, RANKS), jnp.int32),
+            pltpu.VMEM((SLOTS, RANKS), jnp.int32),
             pltpu.SemaphoreType.DMA((RANKS,)),
+            pltpu.SemaphoreType.DMA,
             pltpu.SemaphoreType.DMA((RANKS,)),
+            pltpu.SemaphoreType.DMA,
             pltpu.SemaphoreType.DMA((RANKS,)),
-            pltpu.SemaphoreType.DMA((RANKS,)),
-            pltpu.SemaphoreType.DMA((RANKS,)),
+            pltpu.SemaphoreType.DMA((8,)),
         ],
         compiler_params=pltpu.CompilerParams(
             collective_id=0, has_side_effects=True, vmem_limit_bytes=56 << 20
         ),
     )(
         surface_fields[0], cell_area, remap_tiles.reshape(RANKS, SLOTS, BS, BS),
-        node_block, pair_blocks, cells, cells, node_block, pair_blocks,
+        node_block, pair_blocks, slot_cell[0].T,
     )
-    return out[None]
+    return out.transpose(1, 0, 2)
 
 
 def solution(mesh):

time: 70.5 us -> 67.2 us (0.953)
  Pallas kernels: 67.1 us -> 64.4 us
    pallas_call x1, Pallas kernels: 67.1 us -> 64.4 us  [on_device(): pl.pallas_call(kernel, out_shape=jax.ShapeDtypeStruct((F_F, 1, NCB * BS),...]
    broadcast_in_dim x1 -> x0, local copies, waits for them, and re-layouts: 2.06 us -> none  [on_device(): return out[None]]
    unnamed x0 -> x1, local copies, waits for them, and re-layouts: none -> 1.72 us
where the time goes in v3:
time: 67.2 us; the launch traced here: 66.1 us
  Pallas kernels  64.4 us (96%)
  local copies, waits for them, and re-layouts  1.72 us (3%)
    pallas_call x1, Pallas kernels, on_device(): pl.pallas_call(kernel, out_shape=jax.ShapeDtypeStruct((F_F, 1, NCB * BS),...  64.4 us
    unnamed x1, local copies, waits for them, and re-layouts  1.72 us

profile of v3, /device:TPU:6, one launch (start us, length us, event | category | flops | bytes accessed | tf_op | source)
XLA Modules:
  0.0 66.1 jit_solution(14472254601892824789)
XLA Ops:
  0.0 64.4 %shard_map.64 = f32[20,1,4096]{2,1,0:T(1,128)} custom-call(bf16[40,4096]{1,0:T(8,128)(2,1)} %bitcast.8, f32[1,4096]{1,0:T(1,128)} %area_hbm.1, bf16[64,8,128,128]{3,2,1,0:T(8,128)(2,1)} %bitcast.6, s32[1,512]{1,0:T(1,128)} %nblk_hbm.1, s32[1,64]{1,0:T(1,128)} %pair_hbm.1, s32[8,64]{1,0:T(8,128)} %bitcast.9), custom_call_target="tpu_custom_call" | custom-call | tf_op jit(solution)/shard_map/pallas_call | solution.py:350
  64.4 1.7 %copy.8 = f32[1,20,4096]{2,0,1:T(1,128)} copy(f32[1,20,4096]{2,0,1:T(1,128)} %bitcast.7) | data formatting | bytes 655360

commit v4 on v3

--- a/solution.py
+++ b/solution.py
@@ -24,8 +24,9 @@
 
 
 def offset(k):
-    o = ((k + 1) * 27) & 63
-    return o >> 4, (o >> 2) & 3, o & 3
+    k = k + 1
+    o = (k * 27) & 63
+    return (o >> 2) & 3, o >> 4, o & 3
 
 
 def shifted(home, k, sign):
@@ -130,15 +131,17 @@
             to_ocean(k).start()
             return carry
 
-        def step(k, carry):
-            products(k)
-            to_ocean(k).start()
+        def step(m, carry):
+            for e in range(2):
+                products(AHEAD + 2 * m + e)
+            for e in range(2):
+                to_ocean(AHEAD + 2 * m + e).start()
             return carry
 
         lax.fori_loop(0, AHEAD, ahead, 0)
         pl.semaphore_wait(barrier, RANKS)
         lax.fori_loop(0, AHEAD, release, 0)
-        lax.fori_loop(AHEAD, RANKS, step, 0)
+        lax.fori_loop(0, (RANKS - AHEAD) // 2, step, 0)
 
         def build(i, carry):
             lane = lax.broadcasted_iota(jnp.int32, (1, 256), 1)

time: 67.2 us -> 66.7 us (level)
  Pallas kernels: 64.4 us -> 63.7 us
    pallas_call x1, Pallas kernels: 64.4 us -> 63.7 us  [on_device(): pl.pallas_call(kernel, out_shape=jax.ShapeDtypeStruct((F_F, 1, NCB * BS),...]
where the time goes in v4:
time: 66.7 us; the launch traced here: 65.4 us
  Pallas kernels  63.7 us (96%)
  local copies, waits for them, and re-layouts  1.72 us (3%)
    pallas_call x1, Pallas kernels, on_device(): pl.pallas_call(kernel, out_shape=jax.ShapeDtypeStruct((F_F, 1, NCB * BS),...  63.7 us
    unnamed x1, local copies, waits for them, and re-layouts  1.72 us

profile of v4, /device:TPU:6, one launch (start us, length us, event | category | flops | bytes accessed | tf_op | source)
XLA Modules:
  0.0 65.4 jit_solution(12338813060883312919)
XLA Ops:
  0.0 63.7 %shard_map.64 = f32[20,1,4096]{2,1,0:T(1,128)} custom-call(bf16[40,4096]{1,0:T(8,128)(2,1)} %bitcast.8, f32[1,4096]{1,0:T(1,128)} %area_hbm.1, bf16[64,8,128,128]{3,2,1,0:T(8,128)(2,1)} %bitcast.6, s32[1,512]{1,0:T(1,128)} %nblk_hbm.1, s32[1,64]{1,0:T(1,128)} %pair_hbm.1, s32[8,64]{1,0:T(8,128)} %bitcast.9), custom_call_target="tpu_custom_call" | custom-call | tf_op jit(solution)/shard_map/pallas_call | solution.py:353
  63.7 1.7 %copy.8 = f32[1,20,4096]{2,0,1:T(1,128)} copy(f32[1,20,4096]{2,0,1:T(1,128)} %bitcast.7) | data formatting | bytes 655360

commit v5 on v4

--- a/solution.py
+++ b/solution.py
@@ -70,7 +70,7 @@
         )
         return carry
 
-    lax.fori_loop(0, RANKS, greet, 0)
+    lax.fori_loop(0, RANKS, greet, 0, unroll=8)
     loads = [
         pltpu.make_async_copy(source, target, isem.at[n])
         for n, (source, target) in enumerate(
@@ -96,7 +96,7 @@
             load_tiles(k).start()
             return carry
 
-        lax.fori_loop(0, RANKS, begin, 0)
+        lax.fori_loop(0, RANKS, begin, 0, unroll=8)
         for load in loads:
             load.wait()
 
@@ -342,7 +342,7 @@
             to_atmosphere(k).start()
             return carry
 
-        lax.fori_loop(0, RANKS, send_back, 0)
+        lax.fori_loop(0, RANKS, send_back, 0, unroll=2)
 
         pltpu.make_async_copy(bsbuf, bsbuf, bssem).wait()
 

time: 66.7 us -> 66.4 us (level)
  no operation moved by 1% of the time
where the time goes in v5:
time: 66.4 us; the launch traced here: 65.2 us
  Pallas kernels  63.5 us (96%)
  local copies, waits for them, and re-layouts  1.72 us (3%)
    pallas_call x1, Pallas kernels, on_device(): pl.pallas_call(kernel, out_shape=jax.ShapeDtypeStruct((F_F, 1, NCB * BS),...  63.5 us
    unnamed x1, local copies, waits for them, and re-layouts  1.72 us

profile of v5, /device:TPU:6, one launch (start us, length us, event | category | flops | bytes accessed | tf_op | source)
XLA Modules:
  0.0 65.2 jit_solution(14719784330398463225)
XLA Ops:
  0.0 63.5 %shard_map.64 = f32[20,1,4096]{2,1,0:T(1,128)} custom-call(bf16[40,4096]{1,0:T(8,128)(2,1)} %bitcast.8, f32[1,4096]{1,0:T(1,128)} %area_hbm.1, bf16[64,8,128,128]{3,2,1,0:T(8,128)(2,1)} %bitcast.6, s32[1,512]{1,0:T(1,128)} %nblk_hbm.1, s32[1,64]{1,0:T(1,128)} %pair_hbm.1, s32[8,64]{1,0:T(8,128)} %bitcast.9), custom_call_target="tpu_custom_call" | custom-call | tf_op jit(solution)/shard_map/pallas_call | solution.py:353
  63.5 1.7 %copy.8 = f32[1,20,4096]{2,0,1:T(1,128)} copy(f32[1,20,4096]{2,0,1:T(1,128)} %bitcast.7) | data formatting | bytes 655360
